TPU v7x, 32 devices: a whole 2x2x4 slice. The times are simulated.
32 devices in a mesh: group: 8 (over y, x, core), blk: 4 (over z).
Axes of the slice: x: 2, y: 2, z: 4, core: 2. Of those that a mesh axis runs over, the one named last changes fastest.
Arguments:
- front: float32 [8, 8192, 512], P('group', None, 'blk'), as said below
- child_blocks: float32 [8, 4, 8, 2, 128, 128], P('group', 'blk'), may hold values from -6 to 6
- child_rows: int32 [8, 4, 8, 2, 128], P('group', 'blk'), may hold values from 512 to 8191, as said below
- child_cols: int32 [8, 4, 8, 2, 128], P('group', 'blk'), may hold values from 0 to 127, each once within a row
- child_counts: int32 [8, 4, 8], P('group', 'blk'), may hold values from 0 to 2, as said below
Outputs:
- factors: float32 [8, 8192, 512], P('group', None, 'blk')
- pivots: float32 [8, 256], P('group')
Inputs may be any that keep to these rules, and one draw needn't show every extreme that they name: Rows 0 to 511 of each front form a symmetric matrix whose leading 2 * 128 rows and columns have a positive diagonal that dominates every row of that block; rows from 512 on are unstructured. `child_rows`: the 128 row indices of one slot are distinct and lie at or below row 512. `child_counts`: for every column block some destination group receives 2 live slots from every source group.
All inputs are finite; a program needn't handle non-finite values.
Results may differ from a plain program's by a relative error of at most 0.0003.
Values sent between devices are 32-bit elements; how exact they have to be, the bound alone decides.
No kernel may reach another device: no remote copies, remote signals or barrier semaphores. Data moves between devices by JAX's collectives and lax.ppermute only.
A program may use at most 64 MiB of HBM per device.

v0:
```python
import jax
import jax.numpy as jnp
from jax import lax
from jax.sharding import PartitionSpec as P

PANELS = 2


def from_root(x, axis, root):
    mine = lax.axis_index(axis) == root
    return lax.psum(jnp.where(mine, x, jnp.zeros_like(x)), axis)


def factor_panel(column, start):
    size = column.shape[1]
    square = lax.slice_in_dim(column, start, start + size, axis=0)
    lower_factor = jnp.linalg.cholesky(square)
    diag_root = jnp.diagonal(lower_factor)
    solved = lax.linalg.triangular_solve(
        lower_factor, column, left_side=False, lower=True, transpose_a=True
    )
    solved = solved / diag_root
    row_ids = lax.broadcasted_iota(jnp.int32, solved.shape, 0)
    solved = jnp.where(row_ids >= start, solved, jnp.zeros_like(solved))
    return (solved, diag_root * diag_root)


def per_device(front, child_blocks, child_rows, child_cols, child_counts):
    blocks_in, rows_in, cols_in, counts_in = (
        lax.all_to_all(child_blocks, "group", split_axis=2, concat_axis=0, tiled=True),
        lax.all_to_all(child_rows, "group", split_axis=2, concat_axis=0, tiled=True),
        lax.all_to_all(child_cols, "group", split_axis=2, concat_axis=0, tiled=True),
        lax.all_to_all(child_counts, "group", split_axis=2, concat_axis=0, tiled=True),
    )
    groups = blocks_in.shape[0]
    slots = blocks_in.shape[3]
    width = blocks_in.shape[4]
    flat_blocks = blocks_in.reshape(groups * slots, width, width)
    flat_rows = rows_in.reshape(groups * slots * width)
    flat_cols = cols_in.reshape(groups * slots, width)
    slot_ids = lax.broadcasted_iota(jnp.int32, (groups, slots), 1)
    live = (slot_ids < counts_in.reshape(groups, 1)).reshape(groups * slots)
    masked = jnp.where(live[:, None, None], flat_blocks, jnp.zeros_like(flat_blocks))
    target_ids = lax.broadcasted_iota(jnp.int32, (groups * slots, width, width), 2)
    placement = (flat_cols[:, :, None] == target_ids).astype(jnp.float32)
    placed = jnp.einsum("sij,sjc->sic", masked, placement, precision=lax.Precision.HIGHEST)
    assembled = front[0].at[flat_rows].add(placed.reshape(groups * slots * width, width))
    my_index = lax.axis_index("blk")
    my_start = my_index * width
    pivot_list = []
    for panel in range(PANELS):
        start = panel * width

        def own_factor(column):
            return factor_panel(column, start)

        def empty_factor(column):
            return (jnp.zeros_like(column), jnp.zeros((width,), jnp.float32))

        factor, pivot = lax.cond(my_index == panel, own_factor, empty_factor, assembled)
        factor, pivot = (from_root(factor, "blk", panel), from_root(pivot, "blk", panel))
        my_rows = lax.dynamic_slice_in_dim(factor, my_start, width, 0)
        updated = assembled - jnp.dot(factor * pivot, my_rows.T, precision=lax.Precision.HIGHEST)
        assembled = jnp.where(
            my_index == panel, factor, jnp.where(my_index > panel, updated, assembled)
        )
        pivot_list.append(pivot)
    return (assembled[None], jnp.concatenate(pivot_list)[None])


def solution(mesh):
    in_specs = (
        P("group", None, "blk"),
        P("group", "blk", None, None, None, None),
        P("group", "blk", None, None, None),
        P("group", "blk", None, None, None),
        P("group", "blk", None),
    )
    out_specs = (P("group", None, "blk"), P("group", None))
    return jax.shard_map(
        per_device, mesh=mesh, in_specs=in_specs, out_specs=out_specs, check_vma=False
    )
```

profile of v0, /device:TPU:0, one launch (start us, length us, event | category | flops | bytes accessed | tf_op | source)
XLA Modules:
  0.0 499.8 jit_solution(10520679641883010009)
XLA Ops:
  7.2 4.5 copy.57
  11.7 9.7 %all_to_all.16 = s32[1,1,8]{1,0,2:T(1,128)S(1)} all-to-all(s32[1,1,8]{1,0,2:T(1,128)S(1)} %copy.32), channel_id=1, replica_groups=mesh['group'=8,'blk'=4] {'group'}, dimensions={2} | all-to-all | bytes 64 | tf_op jit(solution)/shard_map/all_to_all | solution.py:33
  21.4 7.1 %all_to_all.17 = s32[1,1,8,2,128]{4,3,1,0,2:T(2,128)S(1)} all-to-all(s32[1,1,8,2,128]{4,3,1,0,2:T(2,128)S(1)} %bitcast.53), channel_id=1, replica_groups=mesh['group'=8,'blk'=4] {'group'}, dimensions={2} | all-to-all | bytes 16384 | tf_op jit(solution)/shard_map/all_to_all | solution.py:31
  28.5 3.6 all-to-all-start.2
  32.5 14.9 %all-to-all-done.2 = f32[1,1,8,2,128,128]{5,4,3,1,0,2:T(8,128)S(1)} async-done(((f32[1,1,8,2,128,128]{5,4,3,1,0,2:T(8,128)}), f32[1,1,8,2,128,128]{5,4,3,1,0,2:T(8,128)S(1)}, u32[]{:S(2)}, u32[]{:S(2)}) %all-to-all-start.2) | async-done | bytes 1048608 | tf_op jit(solution)/shard_map/all_to_all | solution.py:30
  47.4 3.3 all-to-all-start.3
  50.9 4.5 all-to-all-done.3
  56.4 14.5 %scatter_fusion = f32[8192,128]{1,0:T(8,128)} fusion(f32[8192,128]{1,0:T(8,128)} %bitcast.48, s32[2048]{0:T(1024)S(1)} %bitcast.50, f32[2048,128]{1,0:T(8,128)S(1)} %bitcast.49), kind=kCustom, calls=%fused_computation.2 | custom fusion | flops 262144 | bytes 3153920 | tf_op jit(solution)/shard_map/scatter-add | solution.py:47
  71.0 45.7 %conditional.2 = (f32[128]{0:T(128)S(1)}, f32[8192,128]{1,0:T(8,128)}) conditional(s32[]{:T(128)} %convert_element_type.8, () %tuple.27, (f32[8192,128]{1,0:T(8,128)}) %tuple.31), branch_computations={%region_1.2_spmd, %region_2.0_spmd} | conditional | flops 1611809536 | bytes 25957906 | solution.py:60
  71.0 5.6 %copy.41 = f32[8192,128]{0,1:T(8,128)} copy(f32[8192,128]{1,0:T(8,128)} %get-tuple-element.15) | data formatting | bytes 8388608 | tf_op jit(solution)/shard_map/scatter-add | solution.py:47
  78.4 11.7 %cholesky.44 = f32[128,128]{1,0:T(8,128)S(1)} custom-call(f32[128,128]{1,0:T(8,128)S(1)} %fusion.2), custom_call_target="Cholesky" | custom-call | tf_op jit(solution)/shard_map/cond/branch_1_fun/jit(cholesky)/cholesky | solution.py:17
  92.8 9.8 %custom-call.10 = f32[1,128,128]{1,2,0:T(8,128)S(1)} custom-call(f32[1,128,128]{2,1,0:T(8,128)S(1)} %get-tuple-element.18), custom_call_target="InvertDiagBlocksLowerTriangular" | custom-call | tf_op jit(solution)/shard_map/cond/branch_1_fun/triangular_solve/custom-call.0 | solution.py:19
  102.6 8.4 %fusion = f32[8192,128]{0,1:T(8,128)} fusion(f32[8192,128]{1,0:T(8,128)} %get-tuple-element.15, f32[128]{0:T(128)S(1)} %gather_fusion, f32[1,128,128]{1,2,0:T(8,128)S(1)} %custom-call.10), kind=kOutput, calls=%fused_computation.4 | convolution fusion | flops 1611661312 | bytes 8454656 | tf_op jit(solution)/shard_map/cond/branch_1_fun/triangular_solve/dot.3 | solution.py:19
  111.1 5.6 %copy.40 = f32[8192,128]{1,0:T(8,128)} copy(f32[8192,128]{0,1:T(8,128)} %fusion) | data formatting | bytes 8388608 | tf_op jit(solution)/shard_map/cond | solution.py:60
  116.7 4.4 broadcast_select_fusion.1
  121.1 9.0 %psum.29 = f32[128]{0:T(128)S(1)} all-reduce(f32[128]{0:T(128)S(1)} %broadcast_select_fusion.3), channel_id=1, replica_groups=mesh['group'=8,'blk'=4] {'blk'}, use_global_device_ids=true, to_apply=%region_6.9 | all-reduce | flops 128 | bytes 1024 | tf_op jit(solution)/shard_map/psum | solution.py:11
  130.1 142.4 %all-reduce.3.cloned.1.call-done = f32[8192,128]{1,0:T(8,128)} async-done(((f32[8192,128]{1,0:T(8,128)}), f32[8192,128]{1,0:T(8,128)}) %all-reduce.3.cloned.1.call-update) | async-done | bytes 4194320 | tf_op jit(solution)/shard_map/psum | solution.py:11
  272.5 9.5 %fusion.11 = f32[8192,128]{1,0:T(8,128)} fusion(f32[8192,128]{1,0:T(8,128)} %all-reduce.3.cloned.1.call-done, f32[8192,128]{1,0:T(8,128)} %scatter_fusion, f32[128]{0:T(128)S(1)} %psum.29, pred[]{:T(512)S(6)} %gt.6, pred[]{:T(512)S(6)} %eq.11, s32[]{:T(128)S(6)} %select_n.89), kind=kOutput, calls=%fused_computation.33 | convolution fusion | flops 1614807040 | bytes 16843270 | tf_op jit(solution)/shard_map/dot_general | solution.py:63
  282.0 2.2 conditional.3
  282.0 2.2 broadcast.90.clone
  284.2 2.2 broadcast_select_fusion
  286.5 52.5 %psum.31 = f32[128]{0:T(128)S(1)} all-reduce(f32[128]{0:T(128)S(1)} %broadcast_select_fusion.2), channel_id=1, replica_groups=mesh['group'=8,'blk'=4] {'blk'}, use_global_device_ids=true, to_apply=%region_10.13 | all-reduce | flops 128 | bytes 1024 | tf_op jit(solution)/shard_map/psum | solution.py:11
  339.6 143.9 %all-reduce.5.cloned.1.call-done = f32[8192,128]{1,0:T(8,128)} async-done(((f32[8192,128]{1,0:T(8,128)}), f32[8192,128]{1,0:T(8,128)}) %all-reduce.5.cloned.1.call-update) | async-done | bytes 4194320 | tf_op jit(solution)/shard_map/psum | solution.py:11
  483.5 9.5 %fusion.13 = f32[1,8192,128]{2,1,0:T(8,128)} fusion(f32[8192,128]{1,0:T(8,128)} %all-reduce.5.cloned.1.call-done, f32[8192,128]{1,0:T(8,128)} %fusion.11, f32[128]{0:T(128)S(1)} %psum.31, pred[]{:T(512)S(6)} %gt.7, pred[]{:T(512)S(6)} %eq.10, s32[]{:T(128)S(6)} %select_n.89), kind=kOutput, calls=%fused_computation.35 | convolution fusion | flops 1614807040 | bytes 16843270 | tf_op jit(solution)/shard_map/dot_general | solution.py:63
  (28 shorter events, 6.9 us)
Async XLA Ops:
  7.2 14.3 %copy-start = (s32[1,1,8,2,128]{4,3,2,1,0:T(2,128)S(1)}, s32[1,1,8,2,128]{4,3,2,1,0:T(2,128)}, u32[]{:S(2)}) copy-start(s32[1,1,8,2,128]{4,3,2,1,0:T(2,128)} %param.14) | copy-start | bytes 24580
  7.2 4.5 copy-start.1
  28.5 18.9 %all-to-all-start.2 = ((f32[1,1,8,2,128,128]{5,4,3,1,0,2:T(8,128)}), f32[1,1,8,2,128,128]{5,4,3,1,0,2:T(8,128)S(1)}, u32[]{:S(2)}, u32[]{:S(2)}) async-start(f32[1,1,8,2,128,128]{5,4,3,1,0,2:T(8,128)} %bitcast.14), calls=%async_computation.2 | async-start | bytes 2097152 | tf_op jit(solution)/shard_map/all_to_all | solution.py:30
  47.4 8.0 %all-to-all-start.3 = ((s32[1,1,8,2,128]{4,3,1,0,2:T(2,128)}), s32[1,1,8,2,128]{4,3,1,0,2:T(2,128)S(1)}, u32[]{:S(2)}, u32[]{:S(2)}) async-start(s32[1,1,8,2,128]{4,3,1,0,2:T(2,128)} %bitcast.16), calls=%async_computation.3 | async-start | bytes 16384 | tf_op jit(solution)/shard_map/all_to_all | solution.py:32
  50.7 221.8 %all-reduce.3.cloned.1.call-start = ((), (), s32[]{:S(2)}) async-start(), calls=%async_computation.4 | async-start | bytes 8388608 | tf_op jit(solution)/shard_map/psum | solution.py:11
  121.1 362.4 %all-reduce.5.cloned.1.call-start = ((), (), s32[]{:S(2)}) async-start(), calls=%async_computation.5 | async-start | bytes 8388608 | tf_op jit(solution)/shard_map/psum | solution.py:11
Sparse Core Ops, SparseCore 0:
  121.2 151.2 all-reduce.2
  286.6 196.8 all-reduce.4
where the time goes:
time: 501 us; the launch traced here: 500 us
  waiting for transfers between devices  306 us (61%)
  blocking collectives  78.3 us (16%)
  other arithmetic  46 us (9%)
  matrix products  28.5 us (6%)
  local copies, waits for them, and re-layouts  20.3 us (4%)
  between operations  14.1 us (3%)
  starting transfers between devices  6.98 us (1%)
    psum x2, waiting for transfers between devices, from_root(): return lax.psum(jnp.where(mine, x, jnp.zeros_like(x)), axis)  286 us
    psum x2, blocking collectives, from_root(): return lax.psum(jnp.where(mine, x, jnp.zeros_like(x)), axis)  61.5 us
    dot_general x2, matrix products, per_device(): jnp.dot(factor * pivot, my_rows.T, precision=lax.Precision.HIGHEST)  18.9 us
    all_to_all x1, waiting for transfers between devices, per_device(): lax.all_to_all(child_blocks, 'group', split_axis=2, concat_axis=0, tiled=...  14.9 us
    scatter-add x1, other arithmetic, per_device(): front[0].at[flat_rows].add(placed.reshape(groups * slots * width, width))  14.5 us
    another operation x3, other arithmetic, factor_panel(): lower_factor = jnp.linalg.cholesky(square)  12.5 us
    another operation x2, other arithmetic, factor_panel(): lax.linalg.triangular_solve(lower_factor, column, left_side=False, lower=...  10.5 us
  transfers between devices with their start and end apart: 4, of which 4 were waited for; matrix products, arithmetic and copies ran while one was open for 0% of the time, Pallas kernels for 0%

commit v1 on v0

--- a/solution.py
+++ b/solution.py
@@ -8,7 +8,7 @@
 
 def from_root(x, axis, root):
     mine = lax.axis_index(axis) == root
-    return lax.psum(jnp.where(mine, x, jnp.zeros_like(x)), axis)
+    return jnp.sum(lax.all_gather(jnp.where(mine, x, jnp.zeros_like(x)), axis), axis=0)
 
 
 def factor_panel(column, start):

time: 501 us -> 782 us (1.56)
  waiting for transfers between devices: 306 us -> 571 us
  other arithmetic: 46 us -> 64.2 us
    all_gather x0 -> x2, waiting for transfers between devices: none -> 552 us  [from_root(): lax.all_gather(jnp.where(mine, x, jnp.zeros_like(x)), axis)]
    psum x2 -> x0, waiting for transfers between devices: 286 us -> none  [from_root(): return lax.psum(jnp.where(mine, x, jnp.zeros_like(x)), axis)]
    psum x2 -> x0, blocking collectives: 61.5 us -> none  [from_root(): return lax.psum(jnp.where(mine, x, jnp.zeros_like(x)), axis)]
    all_gather x0 -> x2, blocking collectives: none -> 58.9 us  [from_root(): lax.all_gather(jnp.where(mine, x, jnp.zeros_like(x)), axis)]
    reduce_sum x0 -> x4, other arithmetic: none -> 18.2 us  [from_root(): jnp.sum(lax.all_gather(jnp.where(mine, x, jnp.zeros_like(x)), axis), axis=0)]
where the time goes in v1:
time: 782 us; the launch traced here: 781 us
  waiting for transfers between devices  571 us (73%)
  blocking collectives  75.6 us (10%)
  other arithmetic  64.2 us (8%)
  matrix products  28.5 us (4%)
  local copies, waits for them, and re-layouts  20.3 us (3%)
  between operations  14.1 us (2%)
    all_gather x2, waiting for transfers between devices, from_root(): lax.all_gather(jnp.where(mine, x, jnp.zeros_like(x)), axis)  552 us
    all_gather x2, blocking collectives, from_root(): lax.all_gather(jnp.where(mine, x, jnp.zeros_like(x)), axis)  58.9 us
    dot_general x2, matrix products, per_device(): jnp.dot(factor * pivot, my_rows.T, precision=lax.Precision.HIGHEST)  18.9 us
    reduce_sum x4, other arithmetic, from_root(): jnp.sum(lax.all_gather(jnp.where(mine, x, jnp.zeros_like(x)), axis), axis=0)  18.2 us
  transfers between devices with their start and end apart: 4, of which 4 were waited for; matrix products, arithmetic and copies ran while one was open for 0% of the time, Pallas kernels for 0%

profile of v1, /device:TPU:0, one launch (start us, length us, event | category | flops | bytes accessed | tf_op | source)
XLA Modules:
  0.0 780.9 jit_solution(18823258620750015)
XLA Ops:
  7.2 4.5 copy.55
  11.7 9.7 %all_to_all.16 = s32[1,1,8]{1,0,2:T(1,128)S(1)} all-to-all(s32[1,1,8]{1,0,2:T(1,128)S(1)} %copy.32), channel_id=1, replica_groups=mesh['group'=8,'blk'=4] {'group'}, dimensions={2} | all-to-all | bytes 64 | tf_op jit(solution)/shard_map/all_to_all | solution.py:33
  21.4 7.1 all_to_all.17
  28.5 3.6 all-to-all-start.2
  32.5 14.9 %all-to-all-done.2 = f32[1,1,8,2,128,128]{5,4,3,1,0,2:T(8,128)S(1)} async-done(((f32[1,1,8,2,128,128]{5,4,3,1,0,2:T(8,128)}), f32[1,1,8,2,128,128]{5,4,3,1,0,2:T(8,128)S(1)}, u32[]{:S(2)}, u32[]{:S(2)}) %all-to-all-start.2) | async-done | bytes 1048608 | tf_op jit(solution)/shard_map/all_to_all | solution.py:30
  47.4 3.3 all-to-all-start.3
  50.9 4.5 all-to-all-done.3
  56.4 14.5 %scatter_fusion = f32[8192,128]{1,0:T(8,128)} fusion(f32[8192,128]{1,0:T(8,128)} %bitcast.54, s32[2048]{0:T(1024)S(1)} %bitcast.58, f32[2048,128]{1,0:T(8,128)S(1)} %bitcast.57), kind=kCustom, calls=%fused_computation.2 | custom fusion | flops 262144 | bytes 3153920 | tf_op jit(solution)/shard_map/scatter-add | solution.py:47
  71.0 45.7 %conditional.2 = (f32[128]{0:T(128)S(1)}, f32[8192,128]{1,0:T(8,128)}) conditional(s32[]{:T(128)} %convert_element_type.8, () %tuple.27, (f32[8192,128]{1,0:T(8,128)}) %tuple.31), branch_computations={%region_1.2_spmd, %region_2.0_spmd} | conditional | flops 1611809536 | bytes 25957906 | solution.py:60
  71.0 5.6 copy.41
  78.4 11.7 %cholesky.44 = f32[128,128]{1,0:T(8,128)S(1)} custom-call(f32[128,128]{1,0:T(8,128)S(1)} %fusion.2), custom_call_target="Cholesky" | custom-call | tf_op jit(solution)/shard_map/cond/branch_1_fun/jit(cholesky)/cholesky | solution.py:17
  92.8 9.8 %custom-call.10 = f32[1,128,128]{1,2,0:T(8,128)S(1)} custom-call(f32[1,128,128]{2,1,0:T(8,128)S(1)} %get-tuple-element.18), custom_call_target="InvertDiagBlocksLowerTriangular" | custom-call | tf_op jit(solution)/shard_map/cond/branch_1_fun/triangular_solve/custom-call.0 | solution.py:19
  102.6 8.4 %fusion = f32[8192,128]{0,1:T(8,128)} fusion(f32[8192,128]{1,0:T(8,128)} %get-tuple-element.15, f32[128]{0:T(128)S(1)} %gather_fusion, f32[1,128,128]{1,2,0:T(8,128)S(1)} %custom-call.10), kind=kOutput, calls=%fused_computation.4 | convolution fusion | flops 1611661312 | bytes 8454656 | tf_op jit(solution)/shard_map/cond/branch_1_fun/triangular_solve/dot.3 | solution.py:19
  111.1 5.6 copy.40
  116.7 4.4 broadcast_select_fusion.1
  121.1 7.8 all-gather.4
  129.0 275.4 %all-gather.9.cloned.1.call-done = f32[32768,128]{1,0:T(8,128)} async-done(((f32[8192,128]{1,0:T(8,128)}), f32[32768,128]{1,0:T(8,128)}) %all-gather.9.cloned.1.call-update) | async-done | bytes 16777232 | tf_op jit(solution)/shard_map/all_gather | solution.py:11
  404.3 9.1 %reduce_sum.36 = f32[8192,128]{1,0:T(8,128)} reduce(f32[4,8192,128]{2,1,0:T(8,128)} %bitcast.55, f32[]{:T(128)} %constant.68.clone.1), dimensions={0}, to_apply=%region_5.8 | reduce | flops 3145728 | bytes 20971524 | tf_op jit(solution)/shard_map/reduce_sum | solution.py:11
  413.4 9.5 %fusion.11 = f32[8192,128]{1,0:T(8,128)} fusion(f32[8192,128]{1,0:T(8,128)} %reduce_sum.36, f32[8192,128]{1,0:T(8,128)} %scatter_fusion, f32[128]{0:T(128)S(1)} %reduce_sum.37, pred[]{:T(512)S(6)} %gt.6, pred[]{:T(512)S(6)} %eq.11, s32[]{:T(128)S(6)} %select_n.89), kind=kOutput, calls=%fused_computation.33 | convolution fusion | flops 1614807040 | bytes 16843270 | tf_op jit(solution)/shard_map/dot_general | solution.py:63
  422.8 2.2 conditional.3
  427.3 51.1 %all-gather.5 = f32[4,1,128]{2,1,0:T(1,128)S(1)} all-gather(f32[1,1,128]{2,1,0:T(1,128)S(1)} %fusion.23), channel_id=5, replica_groups=mesh['group'=8,'blk'=4] {'blk'}, dimensions={0}, use_global_device_ids=true | all-gather | bytes 2560 | tf_op jit(solution)/shard_map/all_gather | solution.py:11
  479.0 276.5 %all-gather.11.cloned.1.call-done = f32[32768,128]{1,0:T(8,128)} async-done(((f32[8192,128]{1,0:T(8,128)}), f32[32768,128]{1,0:T(8,128)}) %all-gather.11.cloned.1.call-update) | async-done | bytes 16777232 | tf_op jit(solution)/shard_map/all_gather | solution.py:11
  755.5 9.1 %reduce_sum.38 = f32[8192,128]{1,0:T(8,128)} reduce(f32[4,8192,128]{2,1,0:T(8,128)} %bitcast.56, f32[]{:T(128)} %constant.68.clone.1), dimensions={0}, to_apply=%region_9.12 | reduce | flops 3145728 | bytes 20971524 | tf_op jit(solution)/shard_map/reduce_sum | solution.py:11
  764.6 9.5 %fusion.13 = f32[1,8192,128]{2,1,0:T(8,128)} fusion(f32[8192,128]{1,0:T(8,128)} %reduce_sum.38, f32[8192,128]{1,0:T(8,128)} %fusion.11, f32[128]{0:T(128)S(1)} %reduce_sum.39, pred[]{:T(512)S(6)} %gt.7, pred[]{:T(512)S(6)} %eq.10, s32[]{:T(128)S(6)} %select_n.89), kind=kOutput, calls=%fused_computation.35 | convolution fusion | flops 1614807040 | bytes 16843270 | tf_op jit(solution)/shard_map/dot_general | solution.py:63
  (32 shorter events, 11.4 us)
Async XLA Ops:
  7.2 14.3 %copy-start = (s32[1,1,8,2,128]{4,3,2,1,0:T(2,128)S(1)}, s32[1,1,8,2,128]{4,3,2,1,0:T(2,128)}, u32[]{:S(2)}) copy-start(s32[1,1,8,2,128]{4,3,2,1,0:T(2,128)} %param.14) | copy-start | bytes 24580
  7.2 4.5 copy-start.1
  28.5 18.9 %all-to-all-start.2 = ((f32[1,1,8,2,128,128]{5,4,3,1,0,2:T(8,128)}), f32[1,1,8,2,128,128]{5,4,3,1,0,2:T(8,128)S(1)}, u32[]{:S(2)}, u32[]{:S(2)}) async-start(f32[1,1,8,2,128,128]{5,4,3,1,0,2:T(8,128)} %bitcast.14), calls=%async_computation.2 | async-start | bytes 2097152 | tf_op jit(solution)/shard_map/all_to_all | solution.py:30
  47.4 8.0 %all-to-all-start.3 = ((s32[1,1,8,2,128]{4,3,1,0,2:T(2,128)}), s32[1,1,8,2,128]{4,3,1,0,2:T(2,128)S(1)}, u32[]{:S(2)}, u32[]{:S(2)}) async-start(s32[1,1,8,2,128]{4,3,1,0,2:T(2,128)} %bitcast.16), calls=%async_computation.3 | async-start | bytes 16384 | tf_op jit(solution)/shard_map/all_to_all | solution.py:32
  50.7 353.6 %all-gather.9.cloned.1.call-start = ((), (), s32[]{:S(2)}) async-start(), calls=%async_computation.4 | async-start | bytes 20971520 | tf_op jit(solution)/shard_map/all_gather | solution.py:11
  121.1 634.5 %all-gather.11.cloned.1.call-start = ((), (), s32[]{:S(2)}) async-start(), calls=%async_computation.5 | async-start | bytes 20971520 | tf_op jit(solution)/shard_map/all_gather | solution.py:11
Sparse Core Ops, SparseCore 0:
  121.2 283.0 all-gather.8
  427.4 328.0 all-gather.10
